TPU v7x, 256 devices: a whole 4x4x8 slice. The times are simulated.
256 devices in a mesh: slab: 64 (over y, x, z_lo, core), atom: 4 (over z_hi).
Axes of the slice: x: 4, y: 4, z: 8 (z_hi: 4, z_lo: 2; z = z_hi * 2 + z_lo), core: 2. Of those that a mesh axis runs over, the one named last changes fastest.
Arguments:
- cells: int32 [3, 4096, 512], P(None, 'slab', 'atom'), may hold values from 0 to 255, as said below
- fractions: float32 [3, 4096, 512], P(None, 'slab', 'atom'), may hold values from 0 to 1
- charges: float32 [4096, 512], P('slab', 'atom'), may hold values from -3 to 3
- counts: int32 [4096, 4], P('slab', 'atom'), may hold values from 1 to 128, as said below
- box: float32 [3], replicated, may hold values from 192 to 243.2
Outputs:
- kfield: float32 [2, 256, 256, 256], P(None, 'slab', 'atom')
- totals: float32 [7], replicated
Inputs may be any that keep to these rules, and one draw needn't show every extreme that they name: `cells`: for row r (tile r mod 64 of slab r div 64) every slot's z cell lies in the 4 planes from (r div 64) * 4 and its y cell in the 4 rows from (r mod 64) * 4; x anywhere. `counts`: live slots are the first ones of a tile's 128; some tile is full in every draw.
All inputs are finite; a program needn't handle non-finite values.
Results may differ from a plain program's by a relative error of at most 0.000078.
Values sent between devices are 32-bit elements; how exact they have to be, the bound alone decides.
A program may use at most 64 MiB of HBM per device.

v0:
```python
import functools
import math

import jax
import jax.numpy as jnp
import numpy as np
from jax import lax
from jax.experimental import pallas as pl
from jax.experimental.pallas import tpu as pltpu
from jax.sharding import PartitionSpec as P

K = 256
TILES = 64
SLOTS = 128
SLABS = 64
SHARDS = 4
DZ = 4
QUARTER = 64
MAIN = 16
PLANES = 9
ROWS = 88
SHIFT = 10
LANES = SHARDS * SLOTS
beta = 1.25
F32 = jnp.float32
BF16 = jnp.bfloat16
MESH = pl.DeviceIdType.MESH


def tables():
    index = np.arange(K)
    angle = (index[:, None] * index[None, :] % K) * (2.0 * np.pi / K)
    cosine, sine = np.cos(angle), np.sin(angle)
    plain = np.concatenate([cosine, sine], axis=1)
    blocks = []
    for shard in range(SHARDS):
        cols = slice(shard * QUARTER, (shard + 1) * QUARTER)
        blocks += [cosine[:, cols], -sine[:, cols]]
    ordered = np.concatenate(blocks, axis=1)

    def halves(x):
        high = x.astype(np.float32).astype(jnp.bfloat16)
        low = (x - high.astype(np.float64)).astype(np.float32).astype(jnp.bfloat16)
        return np.stack([high, low])

    turn = 2.0 * np.pi * index / K
    modulus = (120.0 / (66.0 + 52.0 * np.cos(turn) + 2.0 * np.cos(2.0 * turn))) ** 2
    folded = np.where(index < K // 2, index, index - K)
    along_rows = np.zeros((K, 128), np.float32)
    along_rows[:, 0] = modulus
    along_rows[:, 1] = folded
    along_lanes = np.zeros((8, K), np.float32)
    along_lanes[0] = modulus
    along_lanes[1] = folded
    return halves(ordered), halves(plain), along_rows, along_lanes


def spline_weights(frac):
    prior = [jnp.ones_like(frac)]
    for order in range(2, 7):
        nxt = []
        for i in range(order):
            point = frac + i
            if i == 0:
                value = point * prior[0]
            elif i == order - 1:
                value = (order - point) * prior[i - 1]
            else:
                value = point * prior[i] + (order - point) * prior[i - 1]
            nxt.append(value * (1.0 / (order - 1)))
        prior = nxt
    return prior


def halved(x):
    high = x.astype(BF16)
    low = (x - high.astype(F32)).astype(BF16)
    return high, low


def dot(a, b):
    return jnp.dot(a, b, preferred_element_type=F32)


def dot_lanes(a, b):
    return lax.dot_general(a, b, (((1,), (1,)), ((), ())), preferred_element_type=F32)


def kernel(
    cells, fractions, charges, counts, box, tx_hbm, t_hbm, rows_const, lanes_const,
    kfield, totals,
    tx, t, send_atoms, atoms, splines, window, x_high, x_low, grid, planes, from_below, from_above,
    x_out, x_in, y_out, z_in, result, part, parts, middle, middles,
    table_sem, atom_send, atom_recv, halo_send, halo_recv, x_send, x_recv,
    y_send, y_recv, out_sem, sum_send, sum_recv, mid_send, mid_recv,
):
    slab = lax.axis_index("slab")
    atom = lax.axis_index("atom")

    barrier = pltpu.get_barrier_semaphore()
    for step in range(1, SHARDS):
        pl.semaphore_signal(barrier, inc=1, device_id=(slab, lax.rem(atom + step, SHARDS)), device_id_type=MESH)

    def greet(step, carry):
        pl.semaphore_signal(barrier, inc=1, device_id=(lax.rem(slab + step, SLABS), atom), device_id_type=MESH)
        return carry

    lax.fori_loop(1, SLABS, greet, 0)
    load_tx = pltpu.make_async_copy(tx_hbm, tx, table_sem.at[0])
    load_t = pltpu.make_async_copy(t_hbm, t, table_sem.at[1])
    load_tx.start()
    load_t.start()

    slot = lax.broadcasted_iota(jnp.int32, (TILES, SLOTS), 1)
    weight = jnp.where(slot < counts[...], charges[...], 0.0)
    fields = [cells[d].astype(F32) for d in range(3)] + [fractions[d] for d in range(3)] + [weight]
    for shard in range(SHARDS):
        edge = []
        for number, field in enumerate(fields):
            first = shard * MAIN
            send_atoms[shard, number] = field[first : first + MAIN]
            after = (first + MAIN) % TILES
            before = (first - 1) % TILES
            edge += [field[after : after + 1], field[before : before + 1]]
        edge += [jnp.zeros((2, SLOTS), F32)]
        send_atoms[shard, 7] = jnp.concatenate(edge, axis=0)
    pl.semaphore_wait(barrier, SHARDS - 1 + SLABS - 1)

    def atom_copy(step):
        peer = lax.rem(atom + step, SHARDS)
        return pltpu.make_async_remote_copy(
            src_ref=send_atoms.at[peer], dst_ref=atoms.at[atom],
            send_sem=atom_send.at[step], recv_sem=atom_recv.at[SHARDS - step],
            device_id=(slab, peer), device_id_type=MESH,
        )

    for step in (2, 1, 3):
        atom_copy(step).start()
    atoms[atom] = send_atoms[atom]
    grid[...] = jnp.zeros_like(grid)
    for step in (1, 3, 2):
        atom_copy(step).wait_recv()

    def gathered(number):
        main = jnp.concatenate([atoms[shard, number] for shard in range(SHARDS)], axis=1)
        edge = jnp.concatenate([atoms[shard, 7, 2 * number : 2 * number + 2] for shard in range(SHARDS)], axis=1)
        return jnp.concatenate([main, edge, jnp.zeros((6, LANES), F32)], axis=0)

    weights = gathered(6)
    for d in range(3):
        for i, value in enumerate(spline_weights(gathered(3 + d))):
            splines[6 * d + i] = value * weights if d == 0 else value
    for d in range(2):
        cell = gathered(d)
        splines[18 + d] = cell - 4.0 * jnp.floor(cell * 0.25) + 5.0
    first = gathered(2) - 2.0
    first = jnp.where(first < 0.0, first + K, first)
    block = jnp.floor(first * (1.0 / 16.0))
    splines[20] = block
    splines[21] = first - 16.0 * block

    row16 = lax.broadcasted_iota(jnp.int32, (16, LANES), 0).astype(F32)
    row24 = lax.broadcasted_iota(jnp.int32, (24, LANES), 0).astype(F32)

    def spread(step, carry):
        tile = step - 1
        at = lax.rem(step + 17, 18)
        base = pl.multiple_of(((step + 1) // 2) * 8, 8)
        offset = (4 * lax.rem(step + 1, 2)).astype(F32)

        def row(number):
            return splines[number, pl.ds(at, 1), :]

        near_z = row(18) - row16
        near_y = (row(19) + offset) - row16
        table_z = jnp.zeros((16, LANES), F32)
        table_y = jnp.zeros((16, LANES), F32)
        for i in range(6):
            table_z = jnp.where(near_z == i, row(i), table_z)
            table_y = jnp.where(near_y == i, row(6 + i), table_y)
        for p in range(PLANES):
            high, low = halved(table_z[p : p + 1] * table_y)
            window[p * 16 : (p + 1) * 16] = high
            window[PLANES * 16 + p * 16 : PLANES * 16 + (p + 1) * 16] = low
        past = row24 - row(21)
        small = jnp.zeros((24, LANES), F32)
        for j in range(6):
            small = jnp.where(past == j, row(12 + 5 - j), small)
        high = small.astype(BF16).astype(F32)
        low = small - high
        where_block = row(20)
        for b in range(16):
            here = where_block == b
            prior = where_block == (b - 1) % 16
            for source, target in ((high, x_high), (low, x_low)):
                top = jnp.where(here, source[0:8], jnp.where(prior, source[16:24], 0.0))
                bottom = jnp.where(here, source[8:16], 0.0)
                target[b * 16 : (b + 1) * 16] = jnp.concatenate([top, bottom], axis=0).astype(BF16)
        double = dot_lanes(window[...], x_high[...])
        single = dot_lanes(window[0 : PLANES * 16], x_low[...])
        out = double[0 : PLANES * 16] + double[PLANES * 16 :] + single
        out = out.reshape(PLANES, 16, K)
        grid[:, pl.ds(base, 16), :] += out
        return carry

    lax.fori_loop(0, 18, spread, 0)

    planes[...] = grid[:, SHIFT : SHIFT + QUARTER, :]
    above = lax.rem(slab + 1, SLABS)
    below = lax.rem(slab + SLABS - 1, SLABS)
    up = pltpu.make_async_remote_copy(
        src_ref=planes.at[pl.ds(6, 3)], dst_ref=from_below,
        send_sem=halo_send.at[0], recv_sem=halo_recv.at[0], device_id=(above, atom), device_id_type=MESH,
    )
    down = pltpu.make_async_remote_copy(
        src_ref=planes.at[pl.ds(0, 2)], dst_ref=from_above,
        send_sem=halo_send.at[1], recv_sem=halo_recv.at[1], device_id=(below, atom), device_id_type=MESH,
    )
    up.start()
    down.start()
    load_tx.wait()
    load_t.wait()

    def x_copy(half, step):
        peer = lax.rem(atom + step, SHARDS)
        return pltpu.make_async_remote_copy(
            src_ref=x_out.at[half, peer], dst_ref=x_in.at[half, atom],
            send_sem=x_send.at[half, step], recv_sem=x_recv.at[half, SHARDS - step],
            device_id=(slab, peer), device_id_type=MESH,
        )

    for half in range(2):
        if half == 0:
            up.wait_recv()
            real = jnp.concatenate([planes[2] + from_below[0], planes[3] + from_below[1]], axis=0)
        else:
            down.wait_recv()
            real = jnp.concatenate([planes[4] + from_below[2] + from_above[0], planes[5] + from_above[1]], axis=0)
        high, low = halved(real)
        out = dot(high, tx[0]) + dot(low, tx[0]) + dot(high, tx[1])
        for shard in range(SHARDS):
            x_out[half, shard] = out[:, shard * 128 : (shard + 1) * 128].reshape(2, QUARTER, 128)
        for step in (2, 1, 3):
            x_copy(half, step).start()
        x_in[half, atom] = x_out[half, atom]

    lane = lax.broadcasted_iota(jnp.int32, (K, 128), 1)
    row8 = lax.broadcasted_iota(jnp.int32, (32, 8, 128), 1)

    def y_copy(half, step):
        peer = lax.rem(slab + step, SLABS)
        return pltpu.make_async_remote_copy(
            src_ref=y_out.at[half, peer // 2, lax.rem(peer, 2)],
            dst_ref=z_in.at[pl.ds(pl.multiple_of(slab * 16 + half * 8, 8), 8)],
            send_sem=y_send.at[half], recv_sem=y_recv.at[half],
            device_id=(peer, atom), device_id_type=MESH,
        )

    for half in range(2):
        for step in (1, 3, 2):
            x_copy(half, step).wait_recv()
        plain, turned = [], []
        for p in range(2):
            f = jnp.concatenate([x_in[half, shard, p] for shard in range(SHARDS)], axis=0)
            g = pltpu.roll(f, 64, 1)
            plain.append(f)
            turned.append(jnp.where(lane < 64, g, -g))
        both = jnp.concatenate([jnp.concatenate(plain, axis=1), jnp.concatenate(turned, axis=1)], axis=0)
        high, low = halved(both)
        out = dot(t[0], high) + dot(t[0], low) + dot(t[1], high)
        y0 = out[:, 0:128].reshape(32, 8, 128)
        y1 = out[:, 128:256].reshape(32, 8, 128)
        y_out[half, :, 0] = jnp.where(row8 < 4, y0, pltpu.roll(y1, 4, 1))
        y_out[half, :, 1] = jnp.where(row8 < 4, pltpu.roll(y0, 4, 1), y1)

        def send(step, carry):
            y_copy(half, step).start()
            return carry

        lax.fori_loop(1, SLABS, send, 0)
        z_in[pl.ds(pl.multiple_of(slab * 16 + half * 8, 8), 8)] = y_out[half, slab // 2, lax.rem(slab, 2)]

    def y_all(half):
        return pltpu.make_async_remote_copy(
            src_ref=z_in.at[pl.ds(0, 8 * (SLABS - 1))], dst_ref=z_in.at[pl.ds(0, 8 * (SLABS - 1))],
            send_sem=y_send.at[half], recv_sem=y_recv.at[half],
            device_id=(above, atom), device_id_type=MESH,
        )

    span_z, span_y, span_x = box[0], box[1], box[2]
    decay = -(math.pi**2) / beta**2
    ones = jnp.ones((8, K), F32)
    m_z = lanes_const[1:2] / (ones[0:1] * span_z)
    part_z = jnp.exp(decay * m_z * m_z) * lanes_const[0:1]
    own_x = rows_const[pl.ds(pl.multiple_of(atom * QUARTER, QUARTER), QUARTER)]
    m_x = own_x[:, 1:2] / (ones[0, 0] * span_x * jnp.ones((QUARTER, 1), F32))
    scale = jnp.ones((QUARTER, 1), F32) / (math.pi * span_z * span_y * span_x * jnp.ones((QUARTER, 1), F32))
    part_x = jnp.exp(decay * m_x * m_x) * own_x[:, 0:1] * scale
    part_xz = part_x * part_z
    msq_xz = m_x * m_x + m_z * m_z
    own_y = rows_const[pl.ds(pl.multiple_of((slab // 2) * 8, 8), 8)]
    kx_at = lax.broadcasted_iota(jnp.int32, (QUARTER, K), 0) + atom * QUARTER
    kz_at = lax.broadcasted_iota(jnp.int32, (QUARTER, K), 1)
    zero_xz = kx_at + kz_at

    for half in range(2):
        y_all(half).wait_recv()

    sums = [jnp.zeros((1, K), F32) for _ in range(7)]
    for ky in range(DZ):
        f = z_in[pl.ds(ky, K, stride=4), :].T
        high, low = halved(f)
        out = dot(high, t[0]) + dot(low, t[0]) + dot(high, t[1])
        real = out[0:QUARTER, 0:K] + out[QUARTER:, K:]
        imag = out[QUARTER:, 0:K] - out[0:QUARTER, K:]
        y_row = jnp.where(lax.rem(slab, 2) == 0, own_y[ky : ky + 1], own_y[ky + 4 : ky + 5])
        m_y = y_row[:, 1:2] / (jnp.ones((1, 1), F32) * span_y)
        part_y = jnp.exp(decay * m_y * m_y) * y_row[:, 0:1]
        msq = msq_xz + m_y * m_y
        anchor = (zero_xz + (slab * DZ + ky)) == 0
        safe = jnp.where(anchor, 1.0, msq)
        theta = jnp.where(anchor, 0.0, part_xz * part_y / safe)
        result[0, ky] = theta * real
        result[1, ky] = theta * imag
        for c in range(2):
            pltpu.make_async_copy(result.at[c, ky], kfield.at[c, ky], out_sem.at[c, ky]).start()
        half_term = 0.5 * theta * (real * real + imag * imag)
        u = half_term * (2.0 * (1.0 - decay * safe) / safe)
        u_z = u * m_z
        down_x = lambda x: jnp.sum(x, axis=0, keepdims=True)
        s_half, s_u = down_x(half_term), down_x(u)
        s_ux, s_uxx = down_x(u * m_x), down_x(u * m_x * m_x)
        s_uz = s_u * m_z
        terms = [
            s_half,
            s_half - s_uz * m_z,
            s_half - s_u * (m_y * m_y),
            s_half - s_uxx,
            -s_uz * m_y,
            -s_ux * m_z,
            -s_ux * m_y,
        ]
        sums = [a + b for a, b in zip(sums, terms)]
    lane_row = lax.broadcasted_iota(jnp.int32, (1, 128), 1)
    packed = jnp.zeros((1, 128), F32)
    for i, value in enumerate(sums):
        packed = jnp.where(lane_row == i, jnp.sum(value, axis=1, keepdims=True), packed)
    part[0] = packed

    def sum_copy(step):
        peer = lax.rem(slab + step, SLABS)
        return pltpu.make_async_remote_copy(
            src_ref=part.at[0], dst_ref=parts.at[slab],
            send_sem=sum_send, recv_sem=sum_recv, device_id=(peer, atom), device_id_type=MESH,
        )

    def sum_start(step, carry):
        sum_copy(step).start()
        return carry

    lax.fori_loop(1, SLABS, sum_start, 0)
    parts[slab] = packed
    sum_all = pltpu.make_async_remote_copy(
        src_ref=parts.at[pl.ds(0, SLABS - 1)], dst_ref=parts.at[pl.ds(0, SLABS - 1)],
        send_sem=sum_send, recv_sem=sum_recv, device_id=(above, atom), device_id_type=MESH,
    )
    sum_all.wait_recv()
    level = jnp.sum(parts[...], axis=0)
    middle[0] = level

    def mid_copy(step):
        peer = lax.rem(atom + step, SHARDS)
        return pltpu.make_async_remote_copy(
            src_ref=middle.at[0], dst_ref=middles.at[atom],
            send_sem=mid_send.at[step], recv_sem=mid_recv.at[SHARDS - step],
            device_id=(slab, peer), device_id_type=MESH,
        )

    for step in (2, 1, 3):
        mid_copy(step).start()
    middles[atom] = level

    for step in range(1, SHARDS):
        atom_copy(step).wait_send()
        for half in range(2):
            x_copy(half, step).wait_send()
    up.wait_send()
    down.wait_send()
    for half in range(2):
        y_all(half).wait_send()
    sum_all.wait_send()
    for ky in range(DZ):
        for c in range(2):
            pltpu.make_async_copy(result.at[c, ky], kfield.at[c, ky], out_sem.at[c, ky]).wait()
    for step in (1, 3, 2):
        mid_copy(step).wait_recv()
    whole = (middles[0] + middles[1]) + (middles[2] + middles[3])
    totals[...] = whole[:, 0:7] * (1.0 / (TILES * SLABS * SLOTS * SHARDS))
    for step in range(1, SHARDS):
        mid_copy(step).wait_send()


def body(cells, fractions, charges, counts, box):
    tx, t, rows_const, lanes_const = tables()
    vmem = pl.BlockSpec(memory_space=pltpu.VMEM)
    smem = pl.BlockSpec(memory_space=pltpu.SMEM)
    anywhere = pl.BlockSpec(memory_space=pl.ANY)
    dma = pltpu.SemaphoreType.DMA
    scratch = [
        pltpu.VMEM((2, K, 2 * K), BF16),
        pltpu.VMEM((2, K, 2 * K), BF16),
        pltpu.VMEM((SHARDS, 8, MAIN, SLOTS), F32),
        pltpu.VMEM((SHARDS, 8, MAIN, SLOTS), F32),
        pltpu.VMEM((22, 24, LANES), F32),
        pltpu.VMEM((2 * PLANES * 16, LANES), BF16),
        pltpu.VMEM((K, LANES), BF16),
        pltpu.VMEM((K, LANES), BF16),
        pltpu.VMEM((PLANES, ROWS, K), F32),
        pltpu.VMEM((PLANES, QUARTER, K), F32),
        pltpu.VMEM((3, QUARTER, K), F32),
        pltpu.VMEM((2, QUARTER, K), F32),
        pltpu.VMEM((2, SHARDS, 2, QUARTER, 128), F32),
        pltpu.VMEM((2, SHARDS, 2, QUARTER, 128), F32),
        pltpu.VMEM((2, SLABS // 2, 2, 8, 128), F32),
        pltpu.VMEM((SLABS * 16, 128), F32),
        pltpu.VMEM((2, DZ, QUARTER, K), F32),
        pltpu.VMEM((1, 1, 128), F32),
        pltpu.VMEM((SLABS, 1, 128), F32),
        pltpu.VMEM((1, 1, 128), F32),
        pltpu.VMEM((SHARDS, 1, 128), F32),
        dma((2,)), dma((SHARDS,)), dma((SHARDS,)), dma((2,)), dma((2,)), dma((2, SHARDS)), dma((2, SHARDS)),
        dma((2,)), dma((2,)), dma((2, DZ)), dma, dma, dma((SHARDS,)), dma((SHARDS,)),
    ]
    kfield, totals = pl.pallas_call(
        kernel,
        name="ewald",
        out_shape=(
            jax.ShapeDtypeStruct((2, DZ, QUARTER, K), F32),
            jax.ShapeDtypeStruct((1, 7), F32),
        ),
        in_specs=[vmem, vmem, vmem, vmem, smem, anywhere, anywhere, vmem, vmem],
        out_specs=(anywhere, vmem),
        scratch_shapes=scratch,
        compiler_params=pltpu.CompilerParams(collective_id=0, has_side_effects=True, vmem_limit_bytes=48 << 20),
    )(cells, fractions, charges, counts, box, tx, t, rows_const, lanes_const)
    return kfield, totals.reshape(7)


def solution(mesh):
    placed = (P(None, "slab", "atom"), P(None, "slab", "atom"), P("slab", "atom"), P("slab", "atom"), P())
    return jax.shard_map(
        body,
        mesh=mesh,
        in_specs=placed,
        out_specs=(P(None, "slab", "atom", None), P()),
        check_vma=False,
    )
```

profile of v0, /device:TPU:1, one launch (start us, length us, event | category | flops | bytes accessed | tf_op | source)
XLA Modules:
  0.0 73.7 jit_solution(5315023059095572075)
XLA Ops:
  0.6 0.0 copy-start.7
  0.6 0.0 copy-start.5
  0.7 0.8 %copy.11.counts = s32[64,1]{1,0:T(8,128)S(1)} copy(s32[64,1]{0,1:T(1,128)} %param.12) | data formatting | bytes 512 | tf_op args[3]
  1.4 0.0 copy-done.7
  1.4 0.0 copy-done.5
  1.4 0.0 copy-start
  1.4 1.0 %copy-done = bf16[2,256,512]{2,1,0:T(8,128)(2,1)S(1)} copy-done((bf16[2,256,512]{2,1,0:T(8,128)(2,1)S(1)}, bf16[2,256,512]{2,1,0:T(8,128)(2,1)}, u32[]{:S(2)}) %copy-start) | copy-done | bytes 524312
  2.5 0.0 copy-start.1
  2.5 1.0 %copy-done.1 = bf16[2,256,512]{2,1,0:T(8,128)(2,1)S(1)} copy-done((bf16[2,256,512]{2,1,0:T(8,128)(2,1)S(1)}, bf16[2,256,512]{2,1,0:T(8,128)(2,1)}, u32[]{:S(2)}) %copy-start.1) | copy-done | bytes 524312
  3.5 0.0 copy-start.2
  3.5 0.9 %copy-done.2 = f32[256,128]{1,0:T(8,128)S(1)} copy-done((f32[256,128]{1,0:T(8,128)S(1)}, f32[256,128]{1,0:T(8,128)}, u32[]{:S(2)}) %copy-start.2) | copy-done | bytes 131096
  4.4 0.0 copy-start.3
  4.4 0.9 %copy-done.3 = s32[3,64,128]{2,1,0:T(8,128)S(1)} copy-done((s32[3,64,128]{2,1,0:T(8,128)S(1)}, s32[3,64,128]{2,1,0:T(8,128)}, u32[]{:S(2)}) %copy-start.3) | copy-done | bytes 98328
  5.3 0.0 copy-start.4
  5.3 0.9 %copy-done.4 = f32[3,64,128]{2,1,0:T(8,128)S(1)} copy-done((f32[3,64,128]{2,1,0:T(8,128)S(1)}, f32[3,64,128]{2,1,0:T(8,128)}, u32[]{:S(2)}) %copy-start.4) | copy-done | bytes 98328
  6.2 0.0 copy-start.6
  6.2 0.7 copy-done.6
  6.9 65.5 %ewald.1 = (f32[2,4,64,256]{3,2,1,0:T(8,128)S(1)}, f32[1,7]{1,0:T(1,128)S(1)}) custom-call(s32[3,64,128]{2,1,0:T(8,128)S(1)} %copy-done.3, f32[3,64,128]{2,1,0:T(8,128)S(1)} %copy-done.4, f32[64,128]{1,0:T(8,128)S(1)} %copy-done.5, s32[64,1]{1,0:T(8,128)S(1)} %copy.11.counts, f32[3]{0:T(128)S(1)} %copy-done.7, bf16[2,256,512]{2,1,0:T(8,128)(2,1)S(1)} %copy-done.1, ...), custom_call_target="tpu_custom_call" | custom-call | tf_op jit(solution)/shard_map/ewald/pallas_call | solution.py:434
  72.4 0.8 %copy.14 = f32[2,4,64,256]{3,2,1,0:T(8,128)} copy(f32[2,4,64,256]{3,2,1,0:T(8,128)S(1)} %get-tuple-element.8) | data formatting | bytes 1048576
  73.2 0.5 copy.15
Async XLA Ops:
  0.6 0.8 %copy-start.7 = (f32[3]{0:T(128)S(1)}, f32[3]{0:T(128)}, u32[]{:S(2)}) copy-start(f32[3]{0:T(128)} %box.1) | copy-start | bytes 40
  0.6 0.8 %copy-start.5 = (f32[64,128]{1,0:T(8,128)S(1)}, f32[64,128]{1,0:T(8,128)}, u32[]{:S(2)}) copy-start(f32[64,128]{1,0:T(8,128)} %charges.1) | copy-start | bytes 98308
  1.4 1.0 %copy-start = (bf16[2,256,512]{2,1,0:T(8,128)(2,1)S(1)}, bf16[2,256,512]{2,1,0:T(8,128)(2,1)}, u32[]{:S(2)}) copy-start(bf16[2,256,512]{2,1,0:T(8,128)(2,1)} %constant.9.clone.t_hbm) | copy-start | bytes 1572868
  2.5 1.0 %copy-start.1 = (bf16[2,256,512]{2,1,0:T(8,128)(2,1)S(1)}, bf16[2,256,512]{2,1,0:T(8,128)(2,1)}, u32[]{:S(2)}) copy-start(bf16[2,256,512]{2,1,0:T(8,128)(2,1)} %constant.8.clone.tx_hbm) | copy-start | bytes 1572868
  3.5 0.9 %copy-start.2 = (f32[256,128]{1,0:T(8,128)S(1)}, f32[256,128]{1,0:T(8,128)}, u32[]{:S(2)}) copy-start(f32[256,128]{1,0:T(8,128)} %constant.10.clone.rows_const) | copy-start | bytes 393220
  4.4 0.9 %copy-start.3 = (s32[3,64,128]{2,1,0:T(8,128)S(1)}, s32[3,64,128]{2,1,0:T(8,128)}, u32[]{:S(2)}) copy-start(s32[3,64,128]{2,1,0:T(8,128)} %cells.1) | copy-start | bytes 294916
  5.3 0.9 %copy-start.4 = (f32[3,64,128]{2,1,0:T(8,128)S(1)}, f32[3,64,128]{2,1,0:T(8,128)}, u32[]{:S(2)}) copy-start(f32[3,64,128]{2,1,0:T(8,128)} %fractions.1) | copy-start | bytes 294916
  6.2 0.7 copy-start.6
where the time goes:
time: 74.1 us; the launch traced here: 73.7 us
  Pallas kernels  65.5 us (88%)
  local copies, waits for them, and re-layouts  7.53 us (10%)
    pallas_call x1, Pallas kernels, body(): pl.pallas_call(kernel, name='ewald', out_shape=(jax.ShapeDtypeStruct((2,...  65.5 us
    unnamed x19, local copies, waits for them, and re-layouts  7.53 us

commit v1 on v0

--- a/solution.py
+++ b/solution.py
@@ -21,6 +21,9 @@
 ROWS = 88
 SHIFT = 10
 LANES = SHARDS * SLOTS
+PIECES = 4
+BLOCKS = ((0, 5), (5, 4), (9, 4), (13, 5))
+DONE = ((0, 8), (8, 16), (24, 16), (40, 24))
 beta = 1.25
 F32 = jnp.float32
 BF16 = jnp.bfloat16
@@ -87,8 +90,9 @@
 
 
 def kernel(
-    cells, fractions, charges, counts, box, tx_hbm, t_hbm, rows_const, lanes_const,
+    cells_hbm, fractions_hbm, charges_hbm, counts_hbm, box, tx_hbm, t_hbm, rows_hbm, lanes_hbm,
     kfield, totals,
+    cells, fractions, charges, counts, rows_const, lanes_const,
     tx, t, send_atoms, atoms, splines, window, x_high, x_low, grid, planes, from_below, from_above,
     x_out, x_in, y_out, z_in, result, part, parts, middle, middles,
     table_sem, atom_send, atom_recv, halo_send, halo_recv, x_send, x_recv,
@@ -97,76 +101,103 @@
     slab = lax.axis_index("slab")
     atom = lax.axis_index("atom")
 
+    def around(place, step, count):
+        peer = place + step
+        return jnp.where(peer >= count, peer - count, peer)
+
+    pairs = [
+        (cells_hbm, cells), (charges_hbm, charges), (counts_hbm, counts), (fractions_hbm, fractions),
+        (tx_hbm, tx), (t_hbm, t), (rows_hbm, rows_const), (lanes_hbm, lanes_const),
+    ]
+    loads = [pltpu.make_async_copy(a, b, table_sem.at[i]) for i, (a, b) in enumerate(pairs)]
+    for load in loads[:4]:
+        load.start()
     barrier = pltpu.get_barrier_semaphore()
     for step in range(1, SHARDS):
-        pl.semaphore_signal(barrier, inc=1, device_id=(slab, lax.rem(atom + step, SHARDS)), device_id_type=MESH)
+        pl.semaphore_signal(barrier, inc=1, device_id=(slab, around(atom, step, SHARDS)), device_id_type=MESH)
 
     def greet(step, carry):
-        pl.semaphore_signal(barrier, inc=1, device_id=(lax.rem(slab + step, SLABS), atom), device_id_type=MESH)
+        pl.semaphore_signal(barrier, inc=1, device_id=(around(slab, step, SLABS), atom), device_id_type=MESH)
         return carry
 
-    lax.fori_loop(1, SLABS, greet, 0)
-    load_tx = pltpu.make_async_copy(tx_hbm, tx, table_sem.at[0])
-    load_t = pltpu.make_async_copy(t_hbm, t, table_sem.at[1])
-    load_tx.start()
-    load_t.start()
+    lax.fori_loop(1, SLABS, greet, 0, unroll=9)
+    for load in loads[4:]:
+        load.start()
+    pending = []
+    for load in loads[:4]:
+        load.wait()
 
     slot = lax.broadcasted_iota(jnp.int32, (TILES, SLOTS), 1)
-    weight = jnp.where(slot < counts[...], charges[...], 0.0)
+    tile_row = lax.broadcasted_iota(jnp.int32, (TILES, TILES), 0)
+    tile_col = lax.broadcasted_iota(jnp.int32, (TILES, TILES), 1)
+    diagonal = jnp.where(tile_row == tile_col, counts[...].astype(F32), 0.0)
+    limit = jnp.sum(diagonal, axis=1, keepdims=True)
+    weight = jnp.where(slot.astype(F32) < limit, charges[...], 0.0)
     fields = [cells[d].astype(F32) for d in range(3)] + [fractions[d] for d in range(3)] + [weight]
+    spare = jnp.zeros((4, SLOTS), F32)
     for shard in range(SHARDS):
-        edge = []
-        for number, field in enumerate(fields):
-            first = shard * MAIN
-            send_atoms[shard, number] = field[first : first + MAIN]
-            after = (first + MAIN) % TILES
-            before = (first - 1) % TILES
-            edge += [field[after : after + 1], field[before : before + 1]]
-        edge += [jnp.zeros((2, SLOTS), F32)]
-        send_atoms[shard, 7] = jnp.concatenate(edge, axis=0)
+        for piece, (start, size) in enumerate(BLOCKS):
+            first = shard * MAIN + 4 * piece
+            cuts = [field[first : first + 4] for field in fields] + [spare]
+            for pair in range(4):
+                send_atoms[shard, start + pair] = jnp.concatenate(cuts[2 * pair : 2 * pair + 2], axis=0)
+            if size == 5:
+                at = (first - 1 if piece == 0 else first + 4) % TILES
+                edge = [field[at : at + 1] for field in fields] + [spare[0:1]]
+                send_atoms[shard, start + 4] = jnp.concatenate(edge, axis=0)
     pl.semaphore_wait(barrier, SHARDS - 1 + SLABS - 1)
 
-    def atom_copy(step):
-        peer = lax.rem(atom + step, SHARDS)
+    def atom_copy(piece, step):
+        start, size = BLOCKS[piece]
+        peer = around(atom, step, SHARDS)
         return pltpu.make_async_remote_copy(
-            src_ref=send_atoms.at[peer], dst_ref=atoms.at[atom],
-            send_sem=atom_send.at[step], recv_sem=atom_recv.at[SHARDS - step],
+            src_ref=send_atoms.at[peer, pl.ds(start, size)], dst_ref=atoms.at[atom, pl.ds(start, size)],
+            send_sem=atom_send.at[piece, step], recv_sem=atom_recv.at[piece, SHARDS - step],
             device_id=(slab, peer), device_id_type=MESH,
         )
 
-    for step in (2, 1, 3):
-        atom_copy(step).start()
+    for piece in range(PIECES):
+        for step in (2, 1, 3):
+            atom_copy(piece, step).start()
+            pending.append(atom_copy(piece, step).wait_send)
     atoms[atom] = send_atoms[atom]
     grid[...] = jnp.zeros_like(grid)
-    for step in (1, 3, 2):
-        atom_copy(step).wait_recv()
-
-    def gathered(number):
-        main = jnp.concatenate([atoms[shard, number] for shard in range(SHARDS)], axis=1)
-        edge = jnp.concatenate([atoms[shard, 7, 2 * number : 2 * number + 2] for shard in range(SHARDS)], axis=1)
-        return jnp.concatenate([main, edge, jnp.zeros((6, LANES), F32)], axis=0)
-
-    weights = gathered(6)
-    for d in range(3):
-        for i, value in enumerate(spline_weights(gathered(3 + d))):
-            splines[6 * d + i] = value * weights if d == 0 else value
-    for d in range(2):
-        cell = gathered(d)
-        splines[18 + d] = cell - 4.0 * jnp.floor(cell * 0.25) + 5.0
-    first = gathered(2) - 2.0
-    first = jnp.where(first < 0.0, first + K, first)
-    block = jnp.floor(first * (1.0 / 16.0))
-    splines[20] = block
-    splines[21] = first - 16.0 * block
+
+    def weigh(piece):
+        start, size = BLOCKS[piece]
+
+        def gathered(number):
+            row = 4 * (number % 2)
+            main = [atoms[shard, start + number // 2, row : row + 4] for shard in range(SHARDS)]
+            parts_of = [jnp.concatenate(main, axis=1)]
+            if size == 5:
+                edge = [atoms[shard, start + 4, number : number + 1] for shard in range(SHARDS)]
+                parts_of.append(jnp.concatenate(edge, axis=1))
+            parts_of.append(jnp.zeros((8 - size, LANES), F32))
+            return jnp.concatenate(parts_of, axis=0)
+
+        rows = slice(8 * piece, 8 * piece + 8)
+        weights = gathered(6)
+        for d in range(3):
+            for i, value in enumerate(spline_weights(gathered(3 + d))):
+                splines[6 * d + i, rows] = value * weights if d == 0 else value
+        for d in range(2):
+            cell = gathered(d)
+            splines[18 + d, rows] = cell - 4.0 * jnp.floor(cell * 0.25) + 5.0
+        first = gathered(2) - 2.0
+        first = jnp.where(first < 0.0, first + K, first)
+        block = jnp.floor(first * (1.0 / 16.0))
+        splines[20, rows] = block
+        splines[21, rows] = first - 16.0 * block
 
     row16 = lax.broadcasted_iota(jnp.int32, (16, LANES), 0).astype(F32)
     row24 = lax.broadcasted_iota(jnp.int32, (24, LANES), 0).astype(F32)
 
-    def spread(step, carry):
-        tile = step - 1
-        at = lax.rem(step + 17, 18)
-        base = pl.multiple_of(((step + 1) // 2) * 8, 8)
-        offset = (4 * lax.rem(step + 1, 2)).astype(F32)
+    def spread(piece, step):
+        tile = jnp.where(step == 4, 4 * piece - 1 if piece == 0 else 4 * piece + 4, 4 * piece + step)
+        at = 8 * piece + step
+        base = pl.multiple_of(((tile + 2) // 2) * 8, 8)
+        offset = (4 * lax.rem(tile + 2, 2)).astype(F32)
 
         def row(number):
             return splines[number, pl.ds(at, 1), :]
@@ -201,54 +232,90 @@
         out = double[0 : PLANES * 16] + double[PLANES * 16 :] + single
         out = out.reshape(PLANES, 16, K)
         grid[:, pl.ds(base, 16), :] += out
-        return carry
-
-    lax.fori_loop(0, 18, spread, 0)
-
-    planes[...] = grid[:, SHIFT : SHIFT + QUARTER, :]
-    above = lax.rem(slab + 1, SLABS)
-    below = lax.rem(slab + SLABS - 1, SLABS)
-    up = pltpu.make_async_remote_copy(
-        src_ref=planes.at[pl.ds(6, 3)], dst_ref=from_below,
-        send_sem=halo_send.at[0], recv_sem=halo_recv.at[0], device_id=(above, atom), device_id_type=MESH,
-    )
-    down = pltpu.make_async_remote_copy(
-        src_ref=planes.at[pl.ds(0, 2)], dst_ref=from_above,
-        send_sem=halo_send.at[1], recv_sem=halo_recv.at[1], device_id=(below, atom), device_id_type=MESH,
-    )
-    up.start()
-    down.start()
-    load_tx.wait()
-    load_t.wait()
-
-    def x_copy(half, step):
-        peer = lax.rem(atom + step, SHARDS)
+
+    above = around(slab, 1, SLABS)
+    below = jnp.where(slab == 0, SLABS - 1, slab - 1)
+
+    def halo_copies(piece):
+        rows = pl.ds(*DONE[piece])
+        up = pltpu.make_async_remote_copy(
+            src_ref=planes.at[pl.ds(6, 3), rows], dst_ref=from_below.at[:, rows],
+            send_sem=halo_send.at[0, piece], recv_sem=halo_recv.at[0, piece],
+            device_id=(above, atom), device_id_type=MESH,
+        )
+        down = pltpu.make_async_remote_copy(
+            src_ref=planes.at[pl.ds(0, 2), rows], dst_ref=from_above.at[:, rows],
+            send_sem=halo_send.at[1, piece], recv_sem=halo_recv.at[1, piece],
+            device_id=(below, atom), device_id_type=MESH,
+        )
+        return up, down
+
+    def spread_piece(piece):
+        for step in (1, 3, 2):
+            atom_copy(piece, step).wait_recv()
+        weigh(piece)
+
+        def one(step, carry):
+            spread(piece, step)
+            return carry
+
+        lax.fori_loop(0, BLOCKS[piece][1], one, 0)
+        start, size = DONE[piece]
+        planes[:, start : start + size, :] = grid[:, SHIFT + start : SHIFT + start + size, :]
+        for copy in halo_copies(piece):
+            copy.start()
+            pending.append(copy.wait_send)
+
+    def x_copy(piece, half, step):
+        rows = pl.ds(*DONE[piece])
+        peer = around(atom, step, SHARDS)
         return pltpu.make_async_remote_copy(
-            src_ref=x_out.at[half, peer], dst_ref=x_in.at[half, atom],
-            send_sem=x_send.at[half, step], recv_sem=x_recv.at[half, SHARDS - step],
+            src_ref=x_out.at[half, peer, :, rows], dst_ref=x_in.at[half, atom, :, rows],
+            send_sem=x_send.at[piece, half, step], recv_sem=x_recv.at[piece, half, SHARDS - step],
             device_id=(slab, peer), device_id_type=MESH,
         )
 
-    for half in range(2):
-        if half == 0:
-            up.wait_recv()
-            real = jnp.concatenate([planes[2] + from_below[0], planes[3] + from_below[1]], axis=0)
-        else:
-            down.wait_recv()
-            real = jnp.concatenate([planes[4] + from_below[2] + from_above[0], planes[5] + from_above[1]], axis=0)
+    def x_piece(piece):
+        start, size = DONE[piece]
+        rows = slice(start, start + size)
+        for copy in halo_copies(piece):
+            copy.wait_recv()
+        real = jnp.concatenate(
+            [
+                planes[2, rows] + from_below[0, rows],
+                planes[3, rows] + from_below[1, rows],
+                planes[4, rows] + from_below[2, rows] + from_above[0, rows],
+                planes[5, rows] + from_above[1, rows],
+            ],
+            axis=0,
+        )
         high, low = halved(real)
         out = dot(high, tx[0]) + dot(low, tx[0]) + dot(high, tx[1])
-        for shard in range(SHARDS):
-            x_out[half, shard] = out[:, shard * 128 : (shard + 1) * 128].reshape(2, QUARTER, 128)
-        for step in (2, 1, 3):
-            x_copy(half, step).start()
-        x_in[half, atom] = x_out[half, atom]
+        for half in range(2):
+            for shard in range(SHARDS):
+                block = out[2 * half * size : 2 * (half + 1) * size, shard * 128 : (shard + 1) * 128]
+                x_out[half, shard, :, rows] = block.reshape(2, size, 128)
+            for step in (2, 1, 3):
+                x_copy(piece, half, step).start()
+                pending.append(x_copy(piece, half, step).wait_send)
+            x_in[half, atom, :, rows] = x_out[half, atom, :, rows]
+
+    spread_piece(0)
+    spread_piece(1)
+    spread_piece(2)
+    for load in loads[4:]:
+        load.wait()
+    x_piece(0)
+    spread_piece(3)
+    x_piece(1)
+    x_piece(2)
+    x_piece(3)
 
     lane = lax.broadcasted_iota(jnp.int32, (K, 128), 1)
     row8 = lax.broadcasted_iota(jnp.int32, (32, 8, 128), 1)
 
     def y_copy(half, step):
-        peer = lax.rem(slab + step, SLABS)
+        peer = around(slab, step, SLABS)
         return pltpu.make_async_remote_copy(
             src_ref=y_out.at[half, peer // 2, lax.rem(peer, 2)],
             dst_ref=z_in.at[pl.ds(pl.multiple_of(slab * 16 + half * 8, 8), 8)],
@@ -257,8 +324,9 @@
         )
 
     for half in range(2):
-        for step in (1, 3, 2):
-            x_copy(half, step).wait_recv()
+        for piece in range(PIECES):
+            for step in (1, 3, 2):
+                x_copy(piece, half, step).wait_recv()
         plain, turned = [], []
         for p in range(2):
             f = jnp.concatenate([x_in[half, shard, p] for shard in range(SHARDS)], axis=0)
@@ -277,7 +345,7 @@
             y_copy(half, step).start()
             return carry
 
-        lax.fori_loop(1, SLABS, send, 0)
+        lax.fori_loop(1, SLABS, send, 0, unroll=9)
         z_in[pl.ds(pl.multiple_of(slab * 16 + half * 8, 8), 8)] = y_out[half, slab // 2, lax.rem(slab, 2)]
 
     def y_all(half):
@@ -287,6 +355,7 @@
             device_id=(above, atom), device_id_type=MESH,
         )
 
+    pending += [y_all(half).wait_send for half in range(2)]
     span_z, span_y, span_x = box[0], box[1], box[2]
     decay = -(math.pi**2) / beta**2
     ones = jnp.ones((8, K), F32)
@@ -323,7 +392,9 @@
         result[0, ky] = theta * real
         result[1, ky] = theta * imag
         for c in range(2):
-            pltpu.make_async_copy(result.at[c, ky], kfield.at[c, ky], out_sem.at[c, ky]).start()
+            put = pltpu.make_async_copy(result.at[c, ky], kfield.at[c, ky], out_sem.at[c, ky])
+            put.start()
+            pending.append(put.wait)
         half_term = 0.5 * theta * (real * real + imag * imag)
         u = half_term * (2.0 * (1.0 - decay * safe) / safe)
         u_z = u * m_z
@@ -348,7 +419,7 @@
     part[0] = packed
 
     def sum_copy(step):
-        peer = lax.rem(slab + step, SLABS)
+        peer = around(slab, step, SLABS)
         return pltpu.make_async_remote_copy(
             src_ref=part.at[0], dst_ref=parts.at[slab],
             send_sem=sum_send, recv_sem=sum_recv, device_id=(peer, atom), device_id_type=MESH,
@@ -358,12 +429,13 @@
         sum_copy(step).start()
         return carry
 
-    lax.fori_loop(1, SLABS, sum_start, 0)
+    lax.fori_loop(1, SLABS, sum_start, 0, unroll=9)
     parts[slab] = packed
     sum_all = pltpu.make_async_remote_copy(
         src_ref=parts.at[pl.ds(0, SLABS - 1)], dst_ref=parts.at[pl.ds(0, SLABS - 1)],
         send_sem=sum_send, recv_sem=sum_recv, device_id=(above, atom), device_id_type=MESH,
     )
+    pending.append(sum_all.wait_send)
     sum_all.wait_recv()
     level = jnp.sum(parts[...], axis=0)
     middle[0] = level
@@ -380,18 +452,8 @@
         mid_copy(step).start()
     middles[atom] = level
 
-    for step in range(1, SHARDS):
-        atom_copy(step).wait_send()
-        for half in range(2):
-            x_copy(half, step).wait_send()
-    up.wait_send()
-    down.wait_send()
-    for half in range(2):
-        y_all(half).wait_send()
-    sum_all.wait_send()
-    for ky in range(DZ):
-        for c in range(2):
-            pltpu.make_async_copy(result.at[c, ky], kfield.at[c, ky], out_sem.at[c, ky]).wait()
+    for wait in pending:
+        wait()
     for step in (1, 3, 2):
         mid_copy(step).wait_recv()
     whole = (middles[0] + middles[1]) + (middles[2] + middles[3])
@@ -405,13 +467,20 @@
     vmem = pl.BlockSpec(memory_space=pltpu.VMEM)
     smem = pl.BlockSpec(memory_space=pltpu.SMEM)
     anywhere = pl.BlockSpec(memory_space=pl.ANY)
+    hbm = pl.BlockSpec(memory_space=pltpu.HBM)
     dma = pltpu.SemaphoreType.DMA
     scratch = [
+        pltpu.VMEM((3, TILES, SLOTS), jnp.int32),
+        pltpu.VMEM((3, TILES, SLOTS), F32),
+        pltpu.VMEM((TILES, SLOTS), F32),
+        pltpu.VMEM((1, TILES), jnp.int32),
+        pltpu.VMEM((K, 128), F32),
+        pltpu.VMEM((8, K), F32),
         pltpu.VMEM((2, K, 2 * K), BF16),
         pltpu.VMEM((2, K, 2 * K), BF16),
-        pltpu.VMEM((SHARDS, 8, MAIN, SLOTS), F32),
-        pltpu.VMEM((SHARDS, 8, MAIN, SLOTS), F32),
-        pltpu.VMEM((22, 24, LANES), F32),
+        pltpu.VMEM((SHARDS, 18, 8, SLOTS), F32),
+        pltpu.VMEM((SHARDS, 18, 8, SLOTS), F32),
+        pltpu.VMEM((22, 8 * PIECES, LANES), F32),
         pltpu.VMEM((2 * PLANES * 16, LANES), BF16),
         pltpu.VMEM((K, LANES), BF16),
         pltpu.VMEM((K, LANES), BF16),
@@ -428,7 +497,8 @@
         pltpu.VMEM((SLABS, 1, 128), F32),
         pltpu.VMEM((1, 1, 128), F32),
         pltpu.VMEM((SHARDS, 1, 128), F32),
-        dma((2,)), dma((SHARDS,)), dma((SHARDS,)), dma((2,)), dma((2,)), dma((2, SHARDS)), dma((2, SHARDS)),
+        dma((8,)), dma((PIECES, SHARDS)), dma((PIECES, SHARDS)), dma((2, PIECES)), dma((2, PIECES)),
+        dma((PIECES, 2, SHARDS)), dma((PIECES, 2, SHARDS)),
         dma((2,)), dma((2,)), dma((2, DZ)), dma, dma, dma((SHARDS,)), dma((SHARDS,)),
     ]
     kfield, totals = pl.pallas_call(
@@ -438,11 +508,11 @@
             jax.ShapeDtypeStruct((2, DZ, QUARTER, K), F32),
             jax.ShapeDtypeStruct((1, 7), F32),
         ),
-        in_specs=[vmem, vmem, vmem, vmem, smem, anywhere, anywhere, vmem, vmem],
+        in_specs=[hbm, hbm, hbm, hbm, smem, hbm, hbm, hbm, hbm],
         out_specs=(anywhere, vmem),
         scratch_shapes=scratch,
-        compiler_params=pltpu.CompilerParams(collective_id=0, has_side_effects=True, vmem_limit_bytes=48 << 20),
-    )(cells, fractions, charges, counts, box, tx, t, rows_const, lanes_const)
+        compiler_params=pltpu.CompilerParams(collective_id=0, has_side_effects=True),
+    )(cells, fractions, charges, counts.reshape(1, TILES), box, tx, t, rows_const, lanes_const)
     return kfield, totals.reshape(7)
 
 

time: 74.1 us -> 64.6 us (0.87)
  local copies, waits for them, and re-layouts: 7.53 us -> 2.38 us
  Pallas kernels: 65.5 us -> 61.4 us
    unnamed x19 -> x4, local copies, waits for them, and re-layouts: 7.53 us -> 2.38 us
    pallas_call x1, Pallas kernels: 65.5 us -> 61.4 us  [body(): pl.pallas_call(kernel, name='ewald', out_shape=(jax.ShapeDtypeStruct((2,...]
where the time goes in v1:
time: 64.6 us; the launch traced here: 64.4 us
  Pallas kernels  61.4 us (95%)
  local copies, waits for them, and re-layouts  2.38 us (4%)
  between operations  0.65 us (1%)
    pallas_call x1, Pallas kernels, body(): pl.pallas_call(kernel, name='ewald', out_shape=(jax.ShapeDtypeStruct((2,...  61.4 us
    unnamed x4, local copies, waits for them, and re-layouts  2.38 us

profile of v1, /device:TPU:1, one launch (start us, length us, event | category | flops | bytes accessed | tf_op | source)
XLA Modules:
  0.0 64.4 jit_solution(15900198014028218026)
XLA Ops:
  0.6 61.4 %ewald.1 = (f32[2,4,64,256]{3,2,1,0:T(8,128)}, f32[1,7]{1,0:T(1,128)}) custom-call(s32[3,64,128]{2,1,0:T(8,128)} %cells_hbm.1, f32[3,64,128]{2,1,0:T(8,128)} %fractions_hbm.1, f32[64,128]{1,0:T(8,128)} %charges_hbm.1, s32[1,64]{1,0:T(1,128)} %bitcast.2, f32[3]{0:T(128)} %box.1, bf16[2,256,512]{2,1,0:T(8,128)(2,1)} %constant.8.clone.tx_hbm, ...), custom_call_target="tpu_custom_call" | custom-call | tf_op jit(solution)/shard_map/ewald/pallas_call | solution.py:504
  62.0 0.0 copy-start
  62.0 1.9 %copy.13 = f32[2,4,64,256]{3,2,1,0:T(8,128)} copy(f32[2,4,64,256]{3,2,1,0:T(8,128)} %get-tuple-element.8) | data formatting | bytes 1048576
  63.9 0.0 copy-done
  63.9 0.5 copy.14
Async XLA Ops:
  62.0 1.9 %copy-start = (f32[1,7]{1,0:T(1,128)S(1)}, f32[1,7]{1,0:T(1,128)}, u32[]{:S(2)}) copy-start(f32[1,7]{1,0:T(1,128)} %get-tuple-element.5) | copy-start | bytes 88

commit v2 on v1

--- a/solution.py
+++ b/solution.py
@@ -23,7 +23,15 @@
 LANES = SHARDS * SLOTS
 PIECES = 4
 BLOCKS = ((0, 5), (5, 4), (9, 4), (13, 5))
+SPREAD = (range(-1, 3), range(3, 7), range(7, 11), range(11, 17))
 DONE = ((0, 8), (8, 16), (24, 16), (40, 24))
+
+
+def distance(mask):
+    return sum((0, 1, 2, 1)[(mask >> low) & 3] for low in (2, 4)) + ((mask >> 1) & 1)
+
+
+FLIPS = sorted(range(1, SLABS), key=lambda mask: -distance(mask))
 beta = 1.25
 F32 = jnp.float32
 BF16 = jnp.bfloat16
@@ -93,7 +101,7 @@
     cells_hbm, fractions_hbm, charges_hbm, counts_hbm, box, tx_hbm, t_hbm, rows_hbm, lanes_hbm,
     kfield, totals,
     cells, fractions, charges, counts, rows_const, lanes_const,
-    tx, t, send_atoms, atoms, splines, window, x_high, x_low, grid, planes, from_below, from_above,
+    tx, t, send_atoms, atoms, splines, windows, x_highs, x_lows, grid, planes, from_below, from_above,
     x_out, x_in, y_out, z_in, result, part, parts, middle, middles,
     table_sem, atom_send, atom_recv, halo_send, halo_recv, x_send, x_recv,
     y_send, y_recv, out_sem, sum_send, sum_recv, mid_send, mid_recv,
@@ -116,11 +124,15 @@
     for step in range(1, SHARDS):
         pl.semaphore_signal(barrier, inc=1, device_id=(slab, around(atom, step, SHARDS)), device_id_type=MESH)
 
-    def greet(step, carry):
-        pl.semaphore_signal(barrier, inc=1, device_id=(around(slab, step, SLABS), atom), device_id_type=MESH)
-        return carry
-
-    lax.fori_loop(1, SLABS, greet, 0, unroll=9)
+    bits = [(1 - 2 * lax.rem(slab // (1 << b), 2)) * (1 << b) for b in range(6)]
+    lower = [sum((bits[b] for b in range(3) if m >> b & 1), slab) for m in range(8)]
+    upper = [sum((bits[b + 3] for b in range(3) if m >> b & 1), 0) for m in range(8)]
+
+    def across(mask):
+        return lower[mask % 8] + upper[mask // 8]
+
+    for mask in FLIPS:
+        pl.semaphore_signal(barrier, inc=1, device_id=(across(mask), atom), device_id_type=MESH)
     for load in loads[4:]:
         load.start()
     pending = []
@@ -177,61 +189,67 @@
             return jnp.concatenate(parts_of, axis=0)
 
         rows = slice(8 * piece, 8 * piece + 8)
+        def within(cell):
+            return cell - DZ * jnp.floor(cell * (1.0 / DZ))
+
         weights = gathered(6)
-        for d in range(3):
-            for i, value in enumerate(spline_weights(gathered(3 + d))):
-                splines[6 * d + i, rows] = value * weights if d == 0 else value
+        along_z = [value * weights for value in spline_weights(gathered(3))]
+        place = within(gathered(0))
+        is_at = [place == c for c in range(DZ)]
+        for p in range(PLANES):
+            value = jnp.zeros((8, LANES), F32)
+            for c in range(DZ):
+                if 0 <= c + 5 - p <= 5:
+                    value = jnp.where(is_at[c], along_z[c + 5 - p], value)
+            splines[p, rows] = value
         for d in range(2):
-            cell = gathered(d)
-            splines[18 + d, rows] = cell - 4.0 * jnp.floor(cell * 0.25) + 5.0
+            for i, value in enumerate(spline_weights(gathered(4 + d))):
+                splines[PLANES + 6 * d + i, rows] = value
+        splines[21, rows] = within(gathered(1)) + 5.0
         first = gathered(2) - 2.0
         first = jnp.where(first < 0.0, first + K, first)
         block = jnp.floor(first * (1.0 / 16.0))
-        splines[20, rows] = block
-        splines[21, rows] = first - 16.0 * block
+        splines[22, rows] = block
+        splines[23, rows] = first - 16.0 * block
 
     row16 = lax.broadcasted_iota(jnp.int32, (16, LANES), 0).astype(F32)
     row24 = lax.broadcasted_iota(jnp.int32, (24, LANES), 0).astype(F32)
 
-    def spread(piece, step):
-        tile = jnp.where(step == 4, 4 * piece - 1 if piece == 0 else 4 * piece + 4, 4 * piece + step)
-        at = 8 * piece + step
-        base = pl.multiple_of(((tile + 2) // 2) * 8, 8)
-        offset = (4 * lax.rem(tile + 2, 2)).astype(F32)
+    def spread(tile):
+        at = {-1: 4, MAIN: 28}.get(tile, 8 * (tile // 4) + tile % 4)
+        base = ((tile + 2) // 2) * 8
+        offset = 4.0 * (tile % 2)
+        window, x_high, x_low = windows.at[tile % 2], x_highs.at[tile % 2], x_lows.at[tile % 2]
 
         def row(number):
-            return splines[number, pl.ds(at, 1), :]
-
-        near_z = row(18) - row16
-        near_y = (row(19) + offset) - row16
-        table_z = jnp.zeros((16, LANES), F32)
+            return splines[number, at : at + 1, :]
+
+        near_y = (row(21) + offset) - row16
         table_y = jnp.zeros((16, LANES), F32)
         for i in range(6):
-            table_z = jnp.where(near_z == i, row(i), table_z)
-            table_y = jnp.where(near_y == i, row(6 + i), table_y)
+            table_y = jnp.where(near_y == i, row(PLANES + i), table_y)
         for p in range(PLANES):
-            high, low = halved(table_z[p : p + 1] * table_y)
+            high, low = halved(row(p) * table_y)
             window[p * 16 : (p + 1) * 16] = high
             window[PLANES * 16 + p * 16 : PLANES * 16 + (p + 1) * 16] = low
-        past = row24 - row(21)
+        past = row24 - row(23)
         small = jnp.zeros((24, LANES), F32)
         for j in range(6):
-            small = jnp.where(past == j, row(12 + 5 - j), small)
-        high = small.astype(BF16).astype(F32)
-        low = small - high
-        where_block = row(20)
+            small = jnp.where(past == j, row(PLANES + 6 + 5 - j), small)
+        small = jnp.concatenate([small, jnp.zeros((8, LANES), F32)], axis=0)
+        high, low = halved(small)
+        where_block = jnp.broadcast_to(row(22), (16, LANES)).astype(BF16)
+        nothing = jnp.zeros((16, LANES), BF16)
+        is_here = [where_block == b for b in range(16)]
         for b in range(16):
-            here = where_block == b
-            prior = where_block == (b - 1) % 16
             for source, target in ((high, x_high), (low, x_low)):
-                top = jnp.where(here, source[0:8], jnp.where(prior, source[16:24], 0.0))
-                bottom = jnp.where(here, source[8:16], 0.0)
-                target[b * 16 : (b + 1) * 16] = jnp.concatenate([top, bottom], axis=0).astype(BF16)
+                after = jnp.where(is_here[(b - 1) % 16], source[16:32], nothing)
+                target[b * 16 : (b + 1) * 16] = jnp.where(is_here[b], source[0:16], after)
         double = dot_lanes(window[...], x_high[...])
         single = dot_lanes(window[0 : PLANES * 16], x_low[...])
         out = double[0 : PLANES * 16] + double[PLANES * 16 :] + single
         out = out.reshape(PLANES, 16, K)
-        grid[:, pl.ds(base, 16), :] += out
+        grid[:, base : base + 16, :] += out
 
     above = around(slab, 1, SLABS)
     below = jnp.where(slab == 0, SLABS - 1, slab - 1)
@@ -255,11 +273,8 @@
             atom_copy(piece, step).wait_recv()
         weigh(piece)
 
-        def one(step, carry):
-            spread(piece, step)
-            return carry
-
-        lax.fori_loop(0, BLOCKS[piece][1], one, 0)
+        for tile in SPREAD[piece]:
+            spread(tile)
         start, size = DONE[piece]
         planes[:, start : start + size, :] = grid[:, SHIFT + start : SHIFT + start + size, :]
         for copy in halo_copies(piece):
@@ -303,10 +318,10 @@
     spread_piece(0)
     spread_piece(1)
     spread_piece(2)
+    spread_piece(3)
     for load in loads[4:]:
         load.wait()
     x_piece(0)
-    spread_piece(3)
     x_piece(1)
     x_piece(2)
     x_piece(3)
@@ -314,10 +329,10 @@
     lane = lax.broadcasted_iota(jnp.int32, (K, 128), 1)
     row8 = lax.broadcasted_iota(jnp.int32, (32, 8, 128), 1)
 
-    def y_copy(half, step):
-        peer = around(slab, step, SLABS)
+    def y_copy(half, mask):
+        peer = across(mask)
         return pltpu.make_async_remote_copy(
-            src_ref=y_out.at[half, peer // 2, lax.rem(peer, 2)],
+            src_ref=y_out.at[half, peer],
             dst_ref=z_in.at[pl.ds(pl.multiple_of(slab * 16 + half * 8, 8), 8)],
             send_sem=y_send.at[half], recv_sem=y_recv.at[half],
             device_id=(peer, atom), device_id_type=MESH,
@@ -338,15 +353,12 @@
         out = dot(t[0], high) + dot(t[0], low) + dot(t[1], high)
         y0 = out[:, 0:128].reshape(32, 8, 128)
         y1 = out[:, 128:256].reshape(32, 8, 128)
-        y_out[half, :, 0] = jnp.where(row8 < 4, y0, pltpu.roll(y1, 4, 1))
-        y_out[half, :, 1] = jnp.where(row8 < 4, pltpu.roll(y0, 4, 1), y1)
-
-        def send(step, carry):
-            y_copy(half, step).start()
-            return carry
-
-        lax.fori_loop(1, SLABS, send, 0, unroll=9)
-        z_in[pl.ds(pl.multiple_of(slab * 16 + half * 8, 8), 8)] = y_out[half, slab // 2, lax.rem(slab, 2)]
+        even = jnp.where(row8 < 4, y0, pltpu.roll(y1, 4, 1))
+        odd = jnp.where(row8 < 4, pltpu.roll(y0, 4, 1), y1)
+        y_out[half] = jnp.stack([even, odd], axis=1).reshape(SLABS, 8, 128)
+        for mask in FLIPS:
+            y_copy(half, mask).start()
+        z_in[pl.ds(pl.multiple_of(slab * 16 + half * 8, 8), 8)] = y_out[half, slab]
 
     def y_all(half):
         return pltpu.make_async_remote_copy(
@@ -418,18 +430,15 @@
         packed = jnp.where(lane_row == i, jnp.sum(value, axis=1, keepdims=True), packed)
     part[0] = packed
 
-    def sum_copy(step):
-        peer = around(slab, step, SLABS)
+    def sum_copy(mask):
+        peer = across(mask)
         return pltpu.make_async_remote_copy(
             src_ref=part.at[0], dst_ref=parts.at[slab],
             send_sem=sum_send, recv_sem=sum_recv, device_id=(peer, atom), device_id_type=MESH,
         )
 
-    def sum_start(step, carry):
-        sum_copy(step).start()
-        return carry
-
-    lax.fori_loop(1, SLABS, sum_start, 0, unroll=9)
+    for mask in FLIPS:
+        sum_copy(mask).start()
     parts[slab] = packed
     sum_all = pltpu.make_async_remote_copy(
         src_ref=parts.at[pl.ds(0, SLABS - 1)], dst_ref=parts.at[pl.ds(0, SLABS - 1)],
@@ -480,17 +489,17 @@
         pltpu.VMEM((2, K, 2 * K), BF16),
         pltpu.VMEM((SHARDS, 18, 8, SLOTS), F32),
         pltpu.VMEM((SHARDS, 18, 8, SLOTS), F32),
-        pltpu.VMEM((22, 8 * PIECES, LANES), F32),
-        pltpu.VMEM((2 * PLANES * 16, LANES), BF16),
-        pltpu.VMEM((K, LANES), BF16),
-        pltpu.VMEM((K, LANES), BF16),
+        pltpu.VMEM((24, 8 * PIECES, LANES), F32),
+        pltpu.VMEM((2, 2 * PLANES * 16, LANES), BF16),
+        pltpu.VMEM((2, K, LANES), BF16),
+        pltpu.VMEM((2, K, LANES), BF16),
         pltpu.VMEM((PLANES, ROWS, K), F32),
         pltpu.VMEM((PLANES, QUARTER, K), F32),
         pltpu.VMEM((3, QUARTER, K), F32),
         pltpu.VMEM((2, QUARTER, K), F32),
         pltpu.VMEM((2, SHARDS, 2, QUARTER, 128), F32),
         pltpu.VMEM((2, SHARDS, 2, QUARTER, 128), F32),
-        pltpu.VMEM((2, SLABS // 2, 2, 8, 128), F32),
+        pltpu.VMEM((2, SLABS, 8, 128), F32),
         pltpu.VMEM((SLABS * 16, 128), F32),
         pltpu.VMEM((2, DZ, QUARTER, K), F32),
         pltpu.VMEM((1, 1, 128), F32),

time: 64.6 us -> 60.7 us (0.940)
  Pallas kernels: 61.4 us -> 57.5 us
    pallas_call x1, Pallas kernels: 61.4 us -> 57.5 us  [body(): pl.pallas_call(kernel, name='ewald', out_shape=(jax.ShapeDtypeStruct((2,...]
where the time goes in v2:
time: 60.7 us; the launch traced here: 60.5 us
  Pallas kernels  57.5 us (95%)
  local copies, waits for them, and re-layouts  2.38 us (4%)
  between operations  0.65 us (1%)
    pallas_call x1, Pallas kernels, body(): pl.pallas_call(kernel, name='ewald', out_shape=(jax.ShapeDtypeStruct((2,...  57.5 us
    unnamed x4, local copies, waits for them, and re-layouts  2.38 us

profile of v2, /device:TPU:1, one launch (start us, length us, event | category | flops | bytes accessed | tf_op | source)
XLA Modules:
  0.0 60.5 jit_solution(18375068383827491875)
XLA Ops:
  0.6 57.5 %ewald.1 = (f32[2,4,64,256]{3,2,1,0:T(8,128)}, f32[1,7]{1,0:T(1,128)}) custom-call(s32[3,64,128]{2,1,0:T(8,128)} %cells_hbm.1, f32[3,64,128]{2,1,0:T(8,128)} %fractions_hbm.1, f32[64,128]{1,0:T(8,128)} %charges_hbm.1, s32[1,64]{1,0:T(1,128)} %bitcast.2, f32[3]{0:T(128)} %box.1, bf16[2,256,512]{2,1,0:T(8,128)(2,1)} %constant.8.clone.tx_hbm, ...), custom_call_target="tpu_custom_call" | custom-call | tf_op jit(solution)/shard_map/ewald/pallas_call | solution.py:513
  58.2 0.0 copy-start
  58.2 1.9 %copy.13 = f32[2,4,64,256]{3,2,1,0:T(8,128)} copy(f32[2,4,64,256]{3,2,1,0:T(8,128)} %get-tuple-element.8) | data formatting | bytes 1048576
  60.0 0.0 copy-done
  60.0 0.5 copy.14
Async XLA Ops:
  58.2 1.9 %copy-start = (f32[1,7]{1,0:T(1,128)S(1)}, f32[1,7]{1,0:T(1,128)}, u32[]{:S(2)}) copy-start(f32[1,7]{1,0:T(1,128)} %get-tuple-element.5) | copy-start | bytes 88

commit v3 on v2

--- a/solution.py
+++ b/solution.py
@@ -102,7 +102,7 @@
     kfield, totals,
     cells, fractions, charges, counts, rows_const, lanes_const,
     tx, t, send_atoms, atoms, splines, windows, x_highs, x_lows, grid, planes, from_below, from_above,
-    x_out, x_in, y_out, z_in, result, part, parts, middle, middles,
+    x_out, x_in, y_out, z_in, thetas, factors, result, part, parts, middle, middles,
     table_sem, atom_send, atom_recv, halo_send, halo_recv, x_send, x_recv,
     y_send, y_recv, out_sem, sum_send, sum_recv, mid_send, mid_recv,
 ):
@@ -310,10 +310,11 @@
             for shard in range(SHARDS):
                 block = out[2 * half * size : 2 * (half + 1) * size, shard * 128 : (shard + 1) * 128]
                 x_out[half, shard, :, rows] = block.reshape(2, size, 128)
-            for step in (2, 1, 3):
-                x_copy(piece, half, step).start()
-                pending.append(x_copy(piece, half, step).wait_send)
-            x_in[half, atom, :, rows] = x_out[half, atom, :, rows]
+
+    def send_x(piece, half):
+        for step in (2, 1, 3):
+            x_copy(piece, half, step).start()
+            pending.append(x_copy(piece, half, step).wait_send)
 
     spread_piece(0)
     spread_piece(1)
@@ -321,10 +322,15 @@
     spread_piece(3)
     for load in loads[4:]:
         load.wait()
-    x_piece(0)
-    x_piece(1)
-    x_piece(2)
+    for piece in range(3):
+        x_piece(piece)
+        send_x(piece, 0)
+    send_x(0, 1)
     x_piece(3)
+    send_x(3, 0)
+    for piece in range(1, PIECES):
+        send_x(piece, 1)
+    x_in[:, atom] = x_out[:, atom]
 
     lane = lax.broadcasted_iota(jnp.int32, (K, 128), 1)
     row8 = lax.broadcasted_iota(jnp.int32, (32, 8, 128), 1)
@@ -384,6 +390,17 @@
     kz_at = lax.broadcasted_iota(jnp.int32, (QUARTER, K), 1)
     zero_xz = kx_at + kz_at
 
+    m_ys = []
+    for ky in range(DZ):
+        y_row = jnp.where(lax.rem(slab, 2) == 0, own_y[ky : ky + 1], own_y[ky + 4 : ky + 5])
+        m_y = y_row[:, 1:2] / (jnp.ones((1, 1), F32) * span_y)
+        part_y = jnp.exp(decay * m_y * m_y) * y_row[:, 0:1]
+        msq = msq_xz + m_y * m_y
+        anchor = (zero_xz + (slab * DZ + ky)) == 0
+        inverse = 1.0 / jnp.where(anchor, 1.0, msq)
+        thetas[ky] = jnp.where(anchor, 0.0, part_xz * part_y * inverse)
+        factors[ky] = inverse - decay
+        m_ys.append(m_y)
     for half in range(2):
         y_all(half).wait_recv()
 
@@ -394,25 +411,19 @@
         out = dot(high, t[0]) + dot(low, t[0]) + dot(high, t[1])
         real = out[0:QUARTER, 0:K] + out[QUARTER:, K:]
         imag = out[QUARTER:, 0:K] - out[0:QUARTER, K:]
-        y_row = jnp.where(lax.rem(slab, 2) == 0, own_y[ky : ky + 1], own_y[ky + 4 : ky + 5])
-        m_y = y_row[:, 1:2] / (jnp.ones((1, 1), F32) * span_y)
-        part_y = jnp.exp(decay * m_y * m_y) * y_row[:, 0:1]
-        msq = msq_xz + m_y * m_y
-        anchor = (zero_xz + (slab * DZ + ky)) == 0
-        safe = jnp.where(anchor, 1.0, msq)
-        theta = jnp.where(anchor, 0.0, part_xz * part_y / safe)
+        theta, m_y = thetas[ky], m_ys[ky]
         result[0, ky] = theta * real
         result[1, ky] = theta * imag
         for c in range(2):
             put = pltpu.make_async_copy(result.at[c, ky], kfield.at[c, ky], out_sem.at[c, ky])
             put.start()
             pending.append(put.wait)
-        half_term = 0.5 * theta * (real * real + imag * imag)
-        u = half_term * (2.0 * (1.0 - decay * safe) / safe)
-        u_z = u * m_z
+        double = theta * (real * real + imag * imag)
+        u = double * factors[ky]
+        u_x = u * m_x
         down_x = lambda x: jnp.sum(x, axis=0, keepdims=True)
-        s_half, s_u = down_x(half_term), down_x(u)
-        s_ux, s_uxx = down_x(u * m_x), down_x(u * m_x * m_x)
+        s_half, s_u = 0.5 * down_x(double), down_x(u)
+        s_ux, s_uxx = down_x(u_x), down_x(u_x * m_x)
         s_uz = s_u * m_z
         terms = [
             s_half,
@@ -501,6 +512,8 @@
         pltpu.VMEM((2, SHARDS, 2, QUARTER, 128), F32),
         pltpu.VMEM((2, SLABS, 8, 128), F32),
         pltpu.VMEM((SLABS * 16, 128), F32),
+        pltpu.VMEM((DZ, QUARTER, K), F32),
+        pltpu.VMEM((DZ, QUARTER, K), F32),
         pltpu.VMEM((2, DZ, QUARTER, K), F32),
         pltpu.VMEM((1, 1, 128), F32),
         pltpu.VMEM((SLABS, 1, 128), F32),

time: 60.7 us -> 59.7 us (0.984)
  Pallas kernels: 57.5 us -> 56.5 us
    pallas_call x1, Pallas kernels: 57.5 us -> 56.5 us  [body(): pl.pallas_call(kernel, name='ewald', out_shape=(jax.ShapeDtypeStruct((2,...]
where the time goes in v3:
time: 59.7 us; the launch traced here: 59.5 us
  Pallas kernels  56.5 us (95%)
  local copies, waits for them, and re-layouts  2.38 us (4%)
  between operations  0.65 us (1%)
    pallas_call x1, Pallas kernels, body(): pl.pallas_call(kernel, name='ewald', out_shape=(jax.ShapeDtypeStruct((2,...  56.5 us
    unnamed x4, local copies, waits for them, and re-layouts  2.38 us

profile of v3, /device:TPU:1, one launch (start us, length us, event | category | flops | bytes accessed | tf_op | source)
XLA Modules:
  0.0 59.5 jit_solution(6824010810206153591)
XLA Ops:
  0.6 56.5 %ewald.1 = (f32[2,4,64,256]{3,2,1,0:T(8,128)}, f32[1,7]{1,0:T(1,128)}) custom-call(s32[3,64,128]{2,1,0:T(8,128)} %cells_hbm.1, f32[3,64,128]{2,1,0:T(8,128)} %fractions_hbm.1, f32[64,128]{1,0:T(8,128)} %charges_hbm.1, s32[1,64]{1,0:T(1,128)} %bitcast.2, f32[3]{0:T(128)} %box.1, bf16[2,256,512]{2,1,0:T(8,128)(2,1)} %constant.8.clone.tx_hbm, ...), custom_call_target="tpu_custom_call" | custom-call | tf_op jit(solution)/shard_map/ewald/pallas_call | solution.py:526
  57.1 0.0 copy-start
  57.1 1.9 %copy.13 = f32[2,4,64,256]{3,2,1,0:T(8,128)} copy(f32[2,4,64,256]{3,2,1,0:T(8,128)} %get-tuple-element.8) | data formatting | bytes 1048576
  59.0 0.0 copy-done
  59.0 0.5 copy.14
Async XLA Ops:
  57.1 1.9 %copy-start = (f32[1,7]{1,0:T(1,128)S(1)}, f32[1,7]{1,0:T(1,128)}, u32[]{:S(2)}) copy-start(f32[1,7]{1,0:T(1,128)} %get-tuple-element.5) | copy-start | bytes 88

commit v4 on v3

--- a/solution.py
+++ b/solution.py
@@ -133,8 +133,6 @@
 
     for mask in FLIPS:
         pl.semaphore_signal(barrier, inc=1, device_id=(across(mask), atom), device_id_type=MESH)
-    for load in loads[4:]:
-        load.start()
     pending = []
     for load in loads[:4]:
         load.wait()
@@ -172,6 +170,8 @@
         for step in (2, 1, 3):
             atom_copy(piece, step).start()
             pending.append(atom_copy(piece, step).wait_send)
+    for load in loads[4:]:
+        load.start()
     atoms[atom] = send_atoms[atom]
     grid[...] = jnp.zeros_like(grid)
 
@@ -404,6 +404,7 @@
     for half in range(2):
         y_all(half).wait_recv()
 
+    puts = []
     sums = [jnp.zeros((1, K), F32) for _ in range(7)]
     for ky in range(DZ):
         f = z_in[pl.ds(ky, K, stride=4), :].T
@@ -415,9 +416,7 @@
         result[0, ky] = theta * real
         result[1, ky] = theta * imag
         for c in range(2):
-            put = pltpu.make_async_copy(result.at[c, ky], kfield.at[c, ky], out_sem.at[c, ky])
-            put.start()
-            pending.append(put.wait)
+            puts.append(pltpu.make_async_copy(result.at[c, ky], kfield.at[c, ky], out_sem.at[c, ky]))
         double = theta * (real * real + imag * imag)
         u = double * factors[ky]
         u_x = u * m_x
@@ -450,6 +449,9 @@
 
     for mask in FLIPS:
         sum_copy(mask).start()
+    for put in puts:
+        put.start()
+        pending.append(put.wait)
     parts[slab] = packed
     sum_all = pltpu.make_async_remote_copy(
         src_ref=parts.at[pl.ds(0, SLABS - 1)], dst_ref=parts.at[pl.ds(0, SLABS - 1)],
@@ -523,6 +525,8 @@
         dma((PIECES, 2, SHARDS)), dma((PIECES, 2, SHARDS)),
         dma((2,)), dma((2,)), dma((2, DZ)), dma, dma, dma((SHARDS,)), dma((SHARDS,)),
     ]
+    arrays = (cells, fractions, charges, counts.reshape(1, TILES), box, tx, t, rows_const, lanes_const)
+    inputs = [pltpu.with_memory_space_constraint(jnp.asarray(x), pltpu.HBM) for x in arrays]
     kfield, totals = pl.pallas_call(
         kernel,
         name="ewald",
@@ -533,8 +537,8 @@
         in_specs=[hbm, hbm, hbm, hbm, smem, hbm, hbm, hbm, hbm],
         out_specs=(anywhere, vmem),
         scratch_shapes=scratch,
-        compiler_params=pltpu.CompilerParams(collective_id=0, has_side_effects=True),
-    )(cells, fractions, charges, counts.reshape(1, TILES), box, tx, t, rows_const, lanes_const)
+        compiler_params=pltpu.CompilerParams(collective_id=0, has_side_effects=True, vmem_limit_bytes=48 << 20),
+    )(*inputs)
     return kfield, totals.reshape(7)
 
 

time: 59.7 us -> 58 us (0.972)
  local copies, waits for them, and re-layouts: 2.38 us -> 1.31 us
  Pallas kernels: 56.5 us -> 55.9 us
    unnamed x4 -> x2, local copies, waits for them, and re-layouts: 2.38 us -> 1.31 us
where the time goes in v4:
time: 58 us; the launch traced here: 57.9 us
  Pallas kernels  55.9 us (96%)
  local copies, waits for them, and re-layouts  1.31 us (2%)
  between operations  0.64 us (1%)
    pallas_call x1, Pallas kernels, body(): pl.pallas_call(kernel, name='ewald', out_shape=(jax.ShapeDtypeStruct((2,...  55.9 us
    unnamed x2, local copies, waits for them, and re-layouts  1.31 us

profile of v4, /device:TPU:1, one launch (start us, length us, event | category | flops | bytes accessed | tf_op | source)
XLA Modules:
  0.0 57.9 jit_solution(5766372612805484779)
XLA Ops:
  0.6 55.9 %ewald.1 = (f32[2,4,64,256]{3,2,1,0:T(8,128)S(1)}, f32[1,7]{1,0:T(1,128)S(1)}) custom-call(s32[3,64,128]{2,1,0:T(8,128)} %cells_hbm.1, f32[3,64,128]{2,1,0:T(8,128)} %fractions_hbm.1, f32[64,128]{1,0:T(8,128)} %charges_hbm.1, s32[1,64]{1,0:T(1,128)} %bitcast.3, f32[3]{0:T(128)} %box.1, bf16[2,256,512]{2,1,0:T(8,128)(2,1)} %constant.8.clone.tx_hbm, ...), custom_call_target="tpu_custom_call" | custom-call | tf_op jit(solution)/shard_map/ewald/pallas_call | solution.py:530
  56.6 0.8 %copy.13 = f32[2,4,64,256]{3,2,1,0:T(8,128)} copy(f32[2,4,64,256]{3,2,1,0:T(8,128)S(1)} %get-tuple-element.8) | data formatting | bytes 1048576
  57.4 0.5 copy.14

commit v5 on v4

--- a/solution.py
+++ b/solution.py
@@ -31,7 +31,7 @@
     return sum((0, 1, 2, 1)[(mask >> low) & 3] for low in (2, 4)) + ((mask >> 1) & 1)
 
 
-FLIPS = sorted(range(1, SLABS), key=lambda mask: -distance(mask))
+FLIPS = sorted(range(1, SLABS), key=lambda mask: (-(mask >> 1 & 1), -distance(mask)))
 beta = 1.25
 F32 = jnp.float32
 BF16 = jnp.bfloat16
@@ -305,7 +305,8 @@
             axis=0,
         )
         high, low = halved(real)
-        out = dot(high, tx[0]) + dot(low, tx[0]) + dot(high, tx[1])
+        double = dot(jnp.concatenate([high, low], axis=0), tx[0])
+        out = double[0 : 4 * size] + double[4 * size :] + dot(high, tx[1])
         for half in range(2):
             for shard in range(SHARDS):
                 block = out[2 * half * size : 2 * (half + 1) * size, shard * 128 : (shard + 1) * 128]
@@ -333,7 +334,7 @@
     x_in[:, atom] = x_out[:, atom]
 
     lane = lax.broadcasted_iota(jnp.int32, (K, 128), 1)
-    row8 = lax.broadcasted_iota(jnp.int32, (32, 8, 128), 1)
+    row8 = lax.broadcasted_iota(jnp.int32, (16, 8, 128), 1)
 
     def y_copy(half, mask):
         peer = across(mask)
@@ -356,14 +357,20 @@
             turned.append(jnp.where(lane < 64, g, -g))
         both = jnp.concatenate([jnp.concatenate(plain, axis=1), jnp.concatenate(turned, axis=1)], axis=0)
         high, low = halved(both)
-        out = dot(t[0], high) + dot(t[0], low) + dot(t[1], high)
-        y0 = out[:, 0:128].reshape(32, 8, 128)
-        y1 = out[:, 128:256].reshape(32, 8, 128)
-        even = jnp.where(row8 < 4, y0, pltpu.roll(y1, 4, 1))
-        odd = jnp.where(row8 < 4, pltpu.roll(y0, 4, 1), y1)
-        y_out[half] = jnp.stack([even, odd], axis=1).reshape(SLABS, 8, 128)
-        for mask in FLIPS:
-            y_copy(half, mask).start()
+        for other in (1, 0):
+            side = slab // 32
+            side = 1 - side if other else side
+            rows = pl.ds(pl.multiple_of(side * 128, 128), 128)
+            t_high, t_low = t[0, rows], t[1, rows]
+            out = dot(t_high, high) + dot(t_high, low) + dot(t_low, high)
+            y0 = out[:, 0:128].reshape(16, 8, 128)
+            y1 = out[:, 128:256].reshape(16, 8, 128)
+            even = jnp.where(row8 < 4, y0, pltpu.roll(y1, 4, 1))
+            odd = jnp.where(row8 < 4, pltpu.roll(y0, 4, 1), y1)
+            y_out[half, pl.ds(side * 32, 32)] = jnp.stack([even, odd], axis=1).reshape(32, 8, 128)
+            for mask in FLIPS:
+                if mask // 32 == other:
+                    y_copy(half, mask).start()
         z_in[pl.ds(pl.multiple_of(slab * 16 + half * 8, 8), 8)] = y_out[half, slab]
 
     def y_all(half):
@@ -409,7 +416,8 @@
     for ky in range(DZ):
         f = z_in[pl.ds(ky, K, stride=4), :].T
         high, low = halved(f)
-        out = dot(high, t[0]) + dot(low, t[0]) + dot(high, t[1])
+        both = dot(jnp.concatenate([high, low], axis=0), t[0])
+        out = both[0:128] + both[128:] + dot(high, t[1])
         real = out[0:QUARTER, 0:K] + out[QUARTER:, K:]
         imag = out[QUARTER:, 0:K] - out[0:QUARTER, K:]
         theta, m_y = thetas[ky], m_ys[ky]

time: 58 us -> 57.7 us (level)
  no operation moved by 1% of the time
where the time goes in v5:
time: 57.7 us; the launch traced here: 57.5 us
  Pallas kernels  55.6 us (96%)
  local copies, waits for them, and re-layouts  1.31 us (2%)
  between operations  0.64 us (1%)
    pallas_call x1, Pallas kernels, body(): pl.pallas_call(kernel, name='ewald', out_shape=(jax.ShapeDtypeStruct((2,...  55.6 us
    unnamed x2, local copies, waits for them, and re-layouts  1.31 us

profile of v5, /device:TPU:1, one launch (start us, length us, event | category | flops | bytes accessed | tf_op | source)
XLA Modules:
  0.0 57.5 jit_solution(473450553441117141)
XLA Ops:
  0.6 55.6 %ewald.1 = (f32[2,4,64,256]{3,2,1,0:T(8,128)S(1)}, f32[1,7]{1,0:T(1,128)S(1)}) custom-call(s32[3,64,128]{2,1,0:T(8,128)} %cells_hbm.1, f32[3,64,128]{2,1,0:T(8,128)} %fractions_hbm.1, f32[64,128]{1,0:T(8,128)} %charges_hbm.1, s32[1,64]{1,0:T(1,128)} %bitcast.3, f32[3]{0:T(128)} %box.1, bf16[2,256,512]{2,1,0:T(8,128)(2,1)} %constant.8.clone.tx_hbm, ...), custom_call_target="tpu_custom_call" | custom-call | tf_op jit(solution)/shard_map/ewald/pallas_call | solution.py:538
  56.2 0.8 %copy.13 = f32[2,4,64,256]{3,2,1,0:T(8,128)} copy(f32[2,4,64,256]{3,2,1,0:T(8,128)S(1)} %get-tuple-element.8) | data formatting | bytes 1048576
  57.0 0.5 copy.14

commit v6 on v5

--- a/solution.py
+++ b/solution.py
@@ -490,6 +490,17 @@
     totals[...] = whole[:, 0:7] * (1.0 / (TILES * SLABS * SLOTS * SHARDS))
     for step in range(1, SHARDS):
         mid_copy(step).wait_send()
+
+
+def put_out(kfield, totals, kfield_out, totals_out, sem):
+    copies = [
+        pltpu.make_async_copy(kfield, kfield_out, sem.at[0]),
+        pltpu.make_async_copy(totals, totals_out, sem.at[1]),
+    ]
+    for copy in copies:
+        copy.start()
+    for copy in copies:
+        copy.wait()
 
 
 def body(cells, fractions, charges, counts, box):
@@ -547,6 +558,18 @@
         scratch_shapes=scratch,
         compiler_params=pltpu.CompilerParams(collective_id=0, has_side_effects=True, vmem_limit_bytes=48 << 20),
     )(*inputs)
+    kfield, totals = pl.pallas_call(
+        put_out,
+        name="put_out",
+        out_shape=(
+            jax.ShapeDtypeStruct((2, DZ, QUARTER, K), F32),
+            jax.ShapeDtypeStruct((1, 7), F32),
+        ),
+        in_specs=[anywhere, anywhere],
+        out_specs=(hbm, hbm),
+        scratch_shapes=[dma((2,))],
+        compiler_params=pltpu.CompilerParams(vmem_limit_bytes=1 << 20),
+    )(kfield, totals)
     return kfield, totals.reshape(7)
 
 

time: 57.7 us -> 57.2 us (level)
  local copies, waits for them, and re-layouts: 1.31 us -> 0 us
  Pallas kernels: 55.6 us -> 56.4 us
    unnamed x2 -> x0, local copies, waits for them, and re-layouts: 1.31 us -> none
    pallas_call x0 -> x1, Pallas kernels: none -> 0.81 us  [body(): pl.pallas_call(put_out, name='put_out', out_shape=(jax.ShapeDtypeStruct((...]
where the time goes in v6:
time: 57.2 us; the launch traced here: 57 us
  Pallas kernels  56.4 us (99%)
  between operations  0.64 us (1%)
    pallas_call x1, Pallas kernels, body(): pl.pallas_call(kernel, name='ewald', out_shape=(jax.ShapeDtypeStruct((2,...  55.6 us

profile of v6, /device:TPU:1, one launch (start us, length us, event | category | flops | bytes accessed | tf_op | source)
XLA Modules:
  0.0 57.0 jit_solution(1526808345447466695)
XLA Ops:
  0.6 55.6 %ewald.1 = (f32[2,4,64,256]{3,2,1,0:T(8,128)S(1)}, f32[1,7]{1,0:T(1,128)S(1)}) custom-call(s32[3,64,128]{2,1,0:T(8,128)} %cells_hbm.1, f32[3,64,128]{2,1,0:T(8,128)} %fractions_hbm.1, f32[64,128]{1,0:T(8,128)} %charges_hbm.1, s32[1,64]{1,0:T(1,128)} %bitcast.2, f32[3]{0:T(128)} %box.1, bf16[2,256,512]{2,1,0:T(8,128)(2,1)} %constant.8.clone.tx_hbm, ...), custom_call_target="tpu_custom_call" | custom-call | tf_op jit(solution)/shard_map/ewald/pallas_call | solution.py:549
  56.2 0.8 %put_out.1 = (f32[2,4,64,256]{3,2,1,0:T(8,128)}, f32[1,7]{1,0:T(1,128)}) custom-call(f32[2,4,64,256]{3,2,1,0:T(8,128)S(1)} %get-tuple-element.6.kfield, f32[1,7]{1,0:T(1,128)S(1)} %get-tuple-element.7.totals), custom_call_target="tpu_custom_call" | custom-call | tf_op jit(solution)/shard_map/put_out/pallas_call | solution.py:561

commit v7 on v6

--- a/solution.py
+++ b/solution.py
@@ -170,8 +170,6 @@
         for step in (2, 1, 3):
             atom_copy(piece, step).start()
             pending.append(atom_copy(piece, step).wait_send)
-    for load in loads[4:]:
-        load.start()
     atoms[atom] = send_atoms[atom]
     grid[...] = jnp.zeros_like(grid)
 
@@ -276,10 +274,12 @@
         for tile in SPREAD[piece]:
             spread(tile)
         start, size = DONE[piece]
-        planes[:, start : start + size, :] = grid[:, SHIFT + start : SHIFT + start + size, :]
-        for copy in halo_copies(piece):
+        ranges = (slice(6, 9), slice(0, 2))
+        for copy, part_of in zip(halo_copies(piece), ranges):
+            planes[part_of, start : start + size, :] = grid[part_of, SHIFT + start : SHIFT + start + size, :]
             copy.start()
             pending.append(copy.wait_send)
+        planes[2:6, start : start + size, :] = grid[2:6, SHIFT + start : SHIFT + start + size, :]
 
     def x_copy(piece, half, step):
         rows = pl.ds(*DONE[piece])
@@ -318,6 +318,8 @@
             pending.append(x_copy(piece, half, step).wait_send)
 
     spread_piece(0)
+    for load in loads[4:]:
+        load.start()
     spread_piece(1)
     spread_piece(2)
     spread_piece(3)

time: 57.2 us -> 57.2 us (level)
  no operation moved by 1% of the time
where the time goes in v7:
time: 57.2 us; the launch traced here: 57.1 us
  Pallas kernels  56.4 us (99%)
  between operations  0.64 us (1%)
    pallas_call x1, Pallas kernels, body(): pl.pallas_call(kernel, name='ewald', out_shape=(jax.ShapeDtypeStruct((2,...  55.6 us

profile of v7, /device:TPU:1, one launch (start us, length us, event | category | flops | bytes accessed | tf_op | source)
XLA Modules:
  0.0 57.1 jit_solution(1367225923790128260)
XLA Ops:
  0.6 55.6 %ewald.1 = (f32[2,4,64,256]{3,2,1,0:T(8,128)S(1)}, f32[1,7]{1,0:T(1,128)S(1)}) custom-call(s32[3,64,128]{2,1,0:T(8,128)} %cells_hbm.1, f32[3,64,128]{2,1,0:T(8,128)} %fractions_hbm.1, f32[64,128]{1,0:T(8,128)} %charges_hbm.1, s32[1,64]{1,0:T(1,128)} %bitcast.2, f32[3]{0:T(128)} %box.1, bf16[2,256,512]{2,1,0:T(8,128)(2,1)} %constant.8.clone.tx_hbm, ...), custom_call_target="tpu_custom_call" | custom-call | tf_op jit(solution)/shard_map/ewald/pallas_call | solution.py:551
  56.3 0.8 %put_out.1 = (f32[2,4,64,256]{3,2,1,0:T(8,128)}, f32[1,7]{1,0:T(1,128)}) custom-call(f32[2,4,64,256]{3,2,1,0:T(8,128)S(1)} %get-tuple-element.6.kfield, f32[1,7]{1,0:T(1,128)S(1)} %get-tuple-element.7.totals), custom_call_target="tpu_custom_call" | custom-call | tf_op jit(solution)/shard_map/put_out/pallas_call | solution.py:563
